TPU v7x, 32 devices: a whole 2x2x4 slice. The times are simulated.
32 devices in a mesh: groups: 2 (over y), frames: 4 (over z), rows: 2 (over x), heads: 2 (over core).
Axes of the slice: x: 2, y: 2, z: 4, core: 2. Of those that a mesh axis runs over, the one named last changes fastest.
Arguments:
- queries: bfloat16 [8, 16, 64, 2240], P(('groups', 'frames'), 'rows', None, 'heads'), parts along dimension 0, may hold values from -2 to 1
- keys: bfloat16 [8, 16, 64, 2240], P(('groups', 'frames'), 'rows', None, 'heads'), parts along dimension 0, may hold values from -6 to 6
- values: bfloat16 [8, 16, 64, 2240], P(('groups', 'frames'), 'rows', None, 'heads'), parts along dimension 0, may hold values from -20 to 20
- out_weight: bfloat16 [2240, 2240], P('heads', 'frames'), may hold values from -0.125 to 0.125
Outputs:
- projected: bfloat16 [8, 16, 64, 2240], P(('groups', 'frames'), 'rows', None, 'heads'), parts along dimension 0
There are 2 independent parts, one for each index of `groups`. A program takes and returns all parts, laid end to end along the dimension named above; an argument that names none is the same for every part. Nothing has to cross between parts.
All inputs are finite; a program needn't handle non-finite values.
Results may differ from a plain program's by a relative error of at most 0.0049.
Values may be sent and summed in bfloat16 or wider, within the bound.
A program may use at most 64 MiB of HBM per device.

v0:
```python
import jax
import jax.numpy as jnp
from jax import lax
from jax.sharding import PartitionSpec as P

HD = 112
EPS = 1e-06


def prefix_before(local):
    position = lax.axis_index("frames") * local[0].shape[0]
    pieces = (
        lax.all_gather(local[0], "frames", axis=0, tiled=True),
        lax.all_gather(local[1], "frames", axis=0, tiled=True),
    )
    count = pieces[0].shape[0]
    keep = jnp.arange(count, dtype=jnp.int32) < position
    states = jnp.sum(jnp.where(keep[:, None, None, None], pieces[0], 0.0), axis=0, keepdims=True)
    totals = jnp.sum(jnp.where(keep[:, None, None], pieces[1], 0.0), axis=0, keepdims=True)
    return (states, totals)


def shards(queries, keys, values, out_weight):
    frames_here, rows_here, columns, features = queries.shape
    heads_here = features // HD
    shape4 = (frames_here, rows_here * columns, heads_here, HD)
    query_pos = jnp.maximum(queries, 0).reshape(shape4).astype(jnp.float32)
    key_pos = jnp.maximum(keys, 0).reshape(shape4)
    value_rows = values.reshape(shape4)
    frame_state = jnp.einsum(
        "fthd,fthe->fhde", key_pos, value_rows, preferred_element_type=jnp.float32
    )
    frame_norm = jnp.sum(key_pos.astype(jnp.float32), axis=1)
    own = lax.psum((frame_state, frame_norm), "rows")
    earlier = prefix_before(own)
    state = own[0] + earlier[0]
    norm = own[1] + earlier[1]
    numer = jnp.einsum("fthd,fhde->fthe", query_pos, state, precision=lax.Precision.HIGHEST)
    denom = jnp.einsum("fthd,fhd->fth", query_pos, norm, precision=lax.Precision.HIGHEST)
    attended = (numer / (denom[..., None] + EPS)).astype(jnp.bfloat16)
    attended = attended.reshape(frames_here * rows_here * columns, features)
    terms = jnp.dot(
        attended,
        lax.all_gather(out_weight, "frames", axis=1, tiled=True),
        preferred_element_type=jnp.float32,
    )
    mixed = lax.psum_scatter(terms, "heads", scatter_dimension=1, tiled=True).astype(jnp.bfloat16)
    return mixed.reshape(frames_here, rows_here, columns, mixed.shape[1])


def solution(mesh):
    return jax.shard_map(
        shards,
        mesh=mesh,
        in_specs=(
            P(("groups", "frames"), "rows", None, "heads"),
            P(("groups", "frames"), "rows", None, "heads"),
            P(("groups", "frames"), "rows", None, "heads"),
            P("heads", "frames"),
        ),
        out_specs=P(("groups", "frames"), "rows", None, "heads"),
        check_vma=False,
    )
```

profile of v0, /device:TPU:0, one launch (start us, length us, event | category | flops | bytes accessed | tf_op | source)
XLA Modules:
  0.0 228.3 jit_solution(10531918947951689015)
XLA Ops:
  6.5 0.0 all-reduce.2.cloned.1.call-start
  6.5 1.4 broadcast_maximum_fusion.1
  7.9 2.5 %reshape.59 = bf16[512,10,112]{2,1,0:T(8,128)(2,1)S(1)} reshape(bf16[1,8,64,1120]{3,2,1,0:T(8,128)(2,1)S(1)} %broadcast_maximum_fusion.1) | data formatting | bytes 2293760 | tf_op jit(solution)/shard_map/reshape
  10.4 4.9 %reshape.60 = bf16[512,10,112]{2,1,0:T(8,128)(2,1)} reshape(bf16[1,8,64,1120]{3,2,1,0:T(8,128)(2,1)} %param.6) | data formatting | bytes 2293760 | tf_op jit(solution)/shard_map/reshape.1
  15.4 3.5 %fusion.4 = f32[1,10,112,112]{3,2,1,0:T(8,128)} fusion(bf16[512,10,112]{2,1,0:T(8,128)(2,1)} %reshape.60, bf16[512,10,112]{2,1,0:T(8,128)(2,1)S(1)} %reshape.59), kind=kOutput, calls=%fused_computation.7 | convolution fusion | flops 128450560 | bytes 2795520 | tf_op jit(solution)/shard_map/fthd,fthe->fhde/dot_general | solution.py:30
  18.9 0.0 copy-start
  18.9 0.0 all-reduce.2.cloned.1.call-update
  18.9 0.0 all-gather.3.cloned.1.call-start
  19.0 32.6 %all-reduce.2.cloned.1.call-done = f32[1,10,112,112]{3,2,1,0:T(8,128)} async-done(((f32[1,10,112,112]{3,2,1,0:T(8,128)}), f32[1,10,112,112]{3,2,1,0:T(8,128)}) %all-reduce.2.cloned.1.call-update) | async-done | bytes 501776 | tf_op jit(solution)/shard_map/psum | solution.py:34
  51.5 0.0 all-gather.3.cloned.1.call-update
  51.6 0.0 all-gather.5.cloned.1.call-start
  51.6 0.7 all-gather.5.cloned.1.call-update
  52.3 0.0 reduce-scatter.2.cloned.1.call-start
  52.3 0.0 copy-done
  52.3 0.3 convert_reduce_fusion
  52.6 0.1 reduce_sum.31
  52.7 1.4 broadcast_maximum_fusion
  54.1 2.5 %reshape.62 = bf16[512,10,112]{2,1,0:T(8,128)(2,1)S(1)} reshape(bf16[1,8,64,1120]{3,2,1,0:T(8,128)(2,1)S(1)} %broadcast_maximum_fusion) | data formatting | bytes 2293760 | tf_op jit(solution)/shard_map/reshape.4
  56.6 1.6 copy.18
  58.2 5.0 %psum.15 = f32[1,10,112]{2,1,0:T(8,128)S(1)} all-reduce(f32[1,10,112]{2,1,0:T(8,128)S(1)} %reduce_sum.31), channel_id=1, replica_groups=mesh['groups'=2,'frames'=4,'rows'=2,'heads'=2] {'rows'}, use_global_device_ids=true, to_apply=%region_3.4 | all-reduce | flops 1120 | bytes 8960 | tf_op jit(solution)/shard_map/psum | solution.py:34
  63.2 13.8 %all_gather.10 = f32[4,10,112]{2,1,0:T(8,128)S(1)} all-gather(f32[1,10,112]{2,1,0:T(8,128)S(1)} %psum.15), channel_id=1, replica_groups=mesh['groups'=2,'frames'=4,'rows'=2,'heads'=2] {'frames'}, dimensions={0}, use_global_device_ids=true | all-gather | bytes 22400 | tf_op jit(solution)/shard_map/all_gather | solution.py:14
  77.0 0.1 select_reduce_fusion.1
  77.1 0.6 fusion.12
  77.6 0.0 copy-start.1
  77.6 24.9 %all-gather.3.cloned.1.call-done = f32[4,10,112,112]{3,2,1,0:T(8,128)} async-done(((f32[1,10,112,112]{3,2,1,0:T(8,128)}), f32[4,10,112,112]{3,2,1,0:T(8,128)}) %all-gather.3.cloned.1.call-update) | async-done | bytes 2007056 | tf_op jit(solution)/shard_map/all_gather | solution.py:13
  102.6 2.0 select_reduce_fusion
  104.6 0.0 copy-done.1
  104.6 2.1 fusion
  106.7 92.8 %all-gather.5.cloned.1.call-done = bf16[1120,2240]{0,1:T(8,128)(2,1)} async-done(((bf16[1120,560]{0,1:T(8,128)(2,1)}), bf16[1120,2240]{0,1:T(8,128)(2,1)}) %all-gather.5.cloned.1.call-update) | async-done | bytes 5017616 | tf_op jit(solution)/shard_map/all_gather | solution.py:44
  199.6 8.1 %fusion.14 = f32[512,2240]{0,1:T(8,128)} fusion(bf16[1120,2240]{0,1:T(8,128)(2,1)} %all-gather.5.cloned.1.call-done, bf16[512,1120]{0,1:T(8,128)(2,1)} %bitcast.45), kind=kOutput, calls=%fused_computation.20 | convolution fusion | flops 2569011200 | bytes 10752000 | tf_op jit(solution)/shard_map/dot_general | solution.py:42
  207.6 0.0 reduce-scatter.2.cloned.1.call-update
  207.7 10.9 %reduce-scatter.2.cloned.1.call-done = f32[512,1120]{0,1:T(8,128)} async-done(((f32[512,2240]{0,1:T(8,128)}), f32[512,1120]{0,1:T(8,128)}) %reduce-scatter.2.cloned.1.call-update) | async-done | bytes 2293776 | tf_op jit(solution)/shard_map/reduce_scatter | solution.py:47
  218.6 1.8 convert_element_type.15
  220.4 1.4 copy.19
  (3 shorter events, 0.0 us)
Async XLA Ops:
  6.5 45.0 %all-reduce.2.cloned.1.call-start = ((), (), s32[]{:S(2)}) async-start(), calls=%async_computation.1 | async-start | bytes 1146880 | tf_op jit(solution)/shard_map/psum | solution.py:34
  18.9 33.4 %copy-start = (bf16[1,8,64,1120]{3,2,1,0:T(8,128)(2,1)S(1)}, bf16[1,8,64,1120]{3,2,1,0:T(8,128)(2,1)}, u32[]{:S(2)}) copy-start(bf16[1,8,64,1120]{3,2,1,0:T(8,128)(2,1)} %param.5) | copy-start | bytes 3440644
  18.9 83.7 %all-gather.3.cloned.1.call-start = ((), (), s32[]{:S(2)}) async-start(), calls=%async_computation.2 | async-start | bytes 2867200 | tf_op jit(solution)/shard_map/all_gather | solution.py:13
  51.6 148.0 %all-gather.5.cloned.1.call-start = ((), (), s32[]{:S(2)}) async-start(), calls=%async_computation.3 | async-start | bytes 6451200 | tf_op jit(solution)/shard_map/all_gather | solution.py:44
  52.3 166.3 %reduce-scatter.2.cloned.1.call-start = ((), (), s32[]{:S(2)}) async-start(), calls=%async_computation.4 | async-start | bytes 6881280 | tf_op jit(solution)/shard_map/reduce_scatter | solution.py:47
  77.6 27.0 %copy-start.1 = (f32[1,10,112,112]{3,2,1,0:T(8,128)S(1)}, f32[1,10,112,112]{3,2,1,0:T(8,128)}, u32[]{:S(2)}) copy-start(f32[1,10,112,112]{3,2,1,0:T(8,128)} %all-reduce.2.cloned.1.call-done) | copy-start | bytes 1505284
Sparse Core Ops, SparseCore 0:
  19.0 32.4 all-reduce.1
  53.1 49.4 all-gather.2
  104.1 95.3 all-gather.4
  207.8 10.7 reduce-scatter.1
where the time goes:
time: 229 us; the launch traced here: 228 us
  waiting for transfers between devices  162 us (71%)
  blocking collectives  18.8 us (8%)
  matrix products  14.3 us (6%)
  between operations  13.2 us (6%)
  local copies, waits for them, and re-layouts  13 us (6%)
  other arithmetic  6.91 us (3%)
    all_gather x1, waiting for transfers between devices, shards(): lax.all_gather(out_weight, 'frames', axis=1, tiled=True)  92.8 us
    psum x1, waiting for transfers between devices, shards(): own = lax.psum((frame_state, frame_norm), 'rows')  32.6 us
    all_gather x1, waiting for transfers between devices, prefix_before(): lax.all_gather(local[0], 'frames', axis=0, tiled=True)  24.9 us
    all_gather x1, blocking collectives, prefix_before(): lax.all_gather(local[1], 'frames', axis=0, tiled=True)  13.8 us
    reduce_scatter x1, waiting for transfers between devices, shards(): lax.psum_scatter(terms, 'heads', scatter_dimension=1, tiled=True)  10.9 us
    another operation x3, local copies, waits for them, and re-layouts  9.01 us
    dot_general x1, matrix products, shards(): jnp.dot(attended, lax.all_gather(out_weight, 'frames', axis=1, tiled=True...  8.06 us
    psum x1, blocking collectives, shards(): own = lax.psum((frame_state, frame_norm), 'rows')  5 us
  transfers between devices with their start and end apart: 4, of which 4 were waited for; matrix products, arithmetic and copies ran while one was open for 5% of the time, Pallas kernels for 0%

commit v1 on v0

--- a/solution.py
+++ b/solution.py
@@ -7,10 +7,22 @@
 EPS = 1e-06
 
 
+def doubled_up(array, axis, dim):
+    ways, here = (lax.axis_size(axis), lax.axis_index(axis))
+    grown, reach = (array, 1)
+    while reach < ways:
+        theirs = lax.ppermute(grown, axis, [(d, d ^ reach) for d in range(ways)])
+        mine_first = jnp.concatenate([grown, theirs], axis=dim)
+        theirs_first = jnp.concatenate([theirs, grown], axis=dim)
+        grown = jnp.where(here & reach == 0, mine_first, theirs_first)
+        reach = 2 * reach
+    return grown
+
+
 def prefix_before(local):
     position = lax.axis_index("frames") * local[0].shape[0]
     pieces = (
-        lax.all_gather(local[0], "frames", axis=0, tiled=True),
+        doubled_up(local[0], "frames", 0),
         lax.all_gather(local[1], "frames", axis=0, tiled=True),
     )
     count = pieces[0].shape[0]

time: 229 us -> 215 us (0.939)
  waiting for transfers between devices: 162 us -> 104 us
  blocking collectives: 18.8 us -> 60.2 us
    all_gather x1, waiting for transfers between devices: 92.8 us -> 0.03 us  [shards(): lax.all_gather(out_weight, 'frames', axis=1, tiled=True)]
    ppermute x0 -> x2, waiting for transfers between devices: none -> 59.9 us  [doubled_up(): theirs = lax.ppermute(grown, axis, [(d, d ^ reach) for d in range(ways)])]
    all_gather x1, blocking collectives: 13.8 us -> 55.2 us  [prefix_before(): lax.all_gather(local[1], 'frames', axis=0, tiled=True)]
    all_gather x1 -> x0, waiting for transfers between devices: 24.9 us -> none  [prefix_before(): lax.all_gather(local[0], 'frames', axis=0, tiled=True)]
  transfers between devices with their start and end apart: 4 -> 5, of which waited for: 4 -> 3; matrix products, arithmetic and copies ran while one was open for 5% -> 5% of each run, Pallas kernels for 0% -> 0%
where the time goes in v1:
time: 215 us
  waiting for transfers between devices  104 us (48%)
  blocking collectives  60.2 us (28%)
  between operations  14.9 us (7%)
  local copies, waits for them, and re-layouts  13 us (6%)
  matrix products  12.6 us (6%)
  other arithmetic  7.88 us (4%)
    ppermute x2, waiting for transfers between devices, doubled_up(): theirs = lax.ppermute(grown, axis, [(d, d ^ reach) for d in range(ways)])  59.9 us
    all_gather x1, blocking collectives, prefix_before(): lax.all_gather(local[1], 'frames', axis=0, tiled=True)  55.2 us
    psum x1, waiting for transfers between devices, shards(): own = lax.psum((frame_state, frame_norm), 'rows')  32 us
    reduce_scatter x1, waiting for transfers between devices, shards(): lax.psum_scatter(terms, 'heads', scatter_dimension=1, tiled=True)  11.9 us
    another operation x3, local copies, waits for them, and re-layouts  8.99 us
    dot_general x1, matrix products, shards(): jnp.dot(attended, lax.all_gather(out_weight, 'frames', axis=1, tiled=True...  7.33 us
    psum x1, blocking collectives, shards(): own = lax.psum((frame_state, frame_norm), 'rows')  5 us
  transfers between devices with their start and end apart: 5, of which 3 were waited for; matrix products, arithmetic and copies ran while one was open for 5% of the time, Pallas kernels for 0%

profile of v1, /device:TPU:0, one launch (start us, length us, event | category | flops | bytes accessed | tf_op | source)
XLA Modules:
  0.0 214.6 jit_solution(15306286023912174771)
XLA Ops:
  7.4 0.0 all-reduce.2.cloned.1.call-start
  7.4 1.4 broadcast_maximum_fusion.1
  8.7 2.5 %reshape.59 = bf16[512,10,112]{2,1,0:T(8,128)(2,1)S(1)} reshape(bf16[1,8,64,1120]{3,2,1,0:T(8,128)(2,1)S(1)} %broadcast_maximum_fusion.1) | data formatting | bytes 2293760 | tf_op jit(solution)/shard_map/reshape
  11.3 4.9 %reshape.60 = bf16[512,10,112]{2,1,0:T(8,128)(2,1)} reshape(bf16[1,8,64,1120]{3,2,1,0:T(8,128)(2,1)} %param.6) | data formatting | bytes 2293760 | tf_op jit(solution)/shard_map/reshape.1
  16.2 3.5 %fusion.6 = f32[1,10,112,112]{3,2,1,0:T(8,128)} fusion(bf16[512,10,112]{2,1,0:T(8,128)(2,1)} %reshape.60, bf16[512,10,112]{2,1,0:T(8,128)(2,1)S(1)} %reshape.59), kind=kOutput, calls=%fused_computation.9 | convolution fusion | flops 128450560 | bytes 2795520 | tf_op jit(solution)/shard_map/fthd,fthe->fhde/dot_general | solution.py:42
  19.7 0.0 copy-start.1
  19.7 0.0 all-reduce.2.cloned.1.call-update
  19.8 0.0 all-gather.2.cloned.1.call-start
  19.8 0.5 all-gather.2.cloned.1.call-update
  20.3 0.0 reduce-scatter.2.cloned.1.call-start
  20.4 32.0 %all-reduce.2.cloned.1.call-done = f32[1,10,112,112]{3,2,1,0:T(8,128)} async-done(((f32[1,10,112,112]{3,2,1,0:T(8,128)}), f32[1,10,112,112]{3,2,1,0:T(8,128)}) %all-reduce.2.cloned.1.call-update) | async-done | bytes 501776 | tf_op jit(solution)/shard_map/psum | solution.py:46
  52.4 0.0 copy-start.2
  52.4 1.5 collective-permute-start
  53.8 0.0 copy-done.1
  53.9 0.1 broadcast_maximum_fusion
  54.0 0.0 copy-start
  54.0 59.9 %collective-permute-done = f32[1,10,112,112]{3,2,1,0:T(8,128)S(1)} collective-permute-done((f32[1,10,112,112]{3,2,1,0:T(8,128)}, f32[1,10,112,112]{3,2,1,0:T(8,128)S(1)}, u32[]{:S(2)}, u32[]{:S(2)}) %collective-permute-start) | collective-permute-done | bytes 501792 | tf_op jit(solution)/shard_map/ppermute | solution.py:14
  113.9 0.0 copy-done.2
  113.9 1.1 maximum_select_fusion.1
  115.0 0.0 collective-permute-start.1
  115.0 0.0 copy-done
  115.0 0.3 convert_reduce_fusion
  115.3 0.1 reduce_sum.31
  115.3 2.5 %reshape.62 = bf16[512,10,112]{2,1,0:T(8,128)(2,1)S(1)} reshape(bf16[1,8,64,1120]{3,2,1,0:T(8,128)(2,1)S(1)} %broadcast_maximum_fusion) | data formatting | bytes 2293760 | tf_op jit(solution)/shard_map/reshape.4
  117.8 1.6 copy.18
  119.4 5.0 %psum.15 = f32[1,10,112]{2,1,0:T(8,128)S(1)} all-reduce(f32[1,10,112]{2,1,0:T(8,128)S(1)} %reduce_sum.31), channel_id=1, replica_groups=mesh['groups'=2,'frames'=4,'rows'=2,'heads'=2] {'rows'}, use_global_device_ids=true, to_apply=%region_3.4 | all-reduce | flops 1120 | bytes 8960 | tf_op jit(solution)/shard_map/psum | solution.py:46
  124.4 55.2 %all_gather.6 = f32[4,10,112]{2,1,0:T(8,128)S(1)} all-gather(f32[1,10,112]{2,1,0:T(8,128)S(1)} %psum.15), channel_id=1, replica_groups=mesh['groups'=2,'frames'=4,'rows'=2,'heads'=2] {'frames'}, dimensions={0}, use_global_device_ids=true | all-gather | bytes 22400 | tf_op jit(solution)/shard_map/all_gather | solution.py:26
  179.6 0.1 select_reduce_fusion
  179.7 0.6 fusion.14
  180.2 0.0 copy-start.3
  180.3 0.0 collective-permute-done.1
  180.3 3.2 %fusion.1 = f32[10,112,112]{2,1,0:T(8,128)S(1)} fusion(f32[2,10,112,112]{3,2,1,0:T(8,128)} %collective-permute-done.1, f32[2,10,112,112]{3,2,1,0:T(8,128)} %maximum_select_fusion.1, pred[4]{0:T(512)(128)(4,1)S(1)} %iota_compare_fusion, pred[]{:T(512)S(6)} %eq.6), kind=kLoop, calls=%fused_computation.3 | loop fusion | flops 2383360 | bytes 2508805 | tf_op jit(solution)/shard_map/reduce_sum | solution.py:30
  183.4 0.0 copy-done.3
  183.4 1.1 fusion.2
  184.6 0.0 all-gather.2.cloned.1.call-done
  184.6 7.3 %fusion.16 = f32[512,2240]{0,1:T(8,128)} fusion(bf16[1120,2240]{0,1:T(8,128)(2,1)} %all-gather.2.cloned.1.call-done, bf16[512,1120]{0,1:T(8,128)(2,1)S(1)} %bitcast.45), kind=kOutput, calls=%fused_computation.23 | convolution fusion | flops 2569011200 | bytes 10752000 | tf_op jit(solution)/shard_map/dot_general | solution.py:54
  191.9 0.0 reduce-scatter.2.cloned.1.call-update
  192.0 11.9 %reduce-scatter.2.cloned.1.call-done = f32[512,1120]{0,1:T(8,128)} async-done(((f32[512,2240]{0,1:T(8,128)}), f32[512,1120]{0,1:T(8,128)}) %reduce-scatter.2.cloned.1.call-update) | async-done | bytes 2293776 | tf_op jit(solution)/shard_map/reduce_scatter | solution.py:59
  203.9 1.8 convert_element_type.15
  205.7 1.4 copy.19
  (3 shorter events, 0.0 us)
Async XLA Ops:
  7.4 45.0 %all-reduce.2.cloned.1.call-start = ((), (), s32[]{:S(2)}) async-start(), calls=%async_computation.1 | async-start | bytes 1146880 | tf_op jit(solution)/shard_map/psum | solution.py:46
  19.7 34.1 %copy-start.1 = (bf16[1,8,64,1120]{3,2,1,0:T(8,128)(2,1)S(1)}, bf16[1,8,64,1120]{3,2,1,0:T(8,128)(2,1)}, u32[]{:S(2)}) copy-start(bf16[1,8,64,1120]{3,2,1,0:T(8,128)(2,1)} %param.4) | copy-start | bytes 3440644
  19.8 164.8 %all-gather.2.cloned.1.call-start = ((), (), s32[]{:S(2)}) async-start(), calls=%async_computation.2 | async-start | bytes 6451200 | tf_op jit(solution)/shard_map/all_gather | solution.py:56
  20.3 183.6 %reduce-scatter.2.cloned.1.call-start = ((), (), s32[]{:S(2)}) async-start(), calls=%async_computation.3 | async-start | bytes 6881280 | tf_op jit(solution)/shard_map/reduce_scatter | solution.py:59
  52.4 61.5 %copy-start.2 = (f32[1,10,112,112]{3,2,1,0:T(8,128)S(1)}, f32[1,10,112,112]{3,2,1,0:T(8,128)}, u32[]{:S(2)}) copy-start(f32[1,10,112,112]{3,2,1,0:T(8,128)} %all-reduce.2.cloned.1.call-done) | copy-start | bytes 1505284
  52.4 61.5 %collective-permute-start = (f32[1,10,112,112]{3,2,1,0:T(8,128)}, f32[1,10,112,112]{3,2,1,0:T(8,128)S(1)}, u32[]{:S(2)}, u32[]{:S(2)}) collective-permute-start(f32[1,10,112,112]{3,2,1,0:T(8,128)} %all-reduce.2.cloned.1.call-done), channel_id=1, source_target_pairs={{0,4},{4,0},{8,12},{12,8},{1,5},{5,1},{9,13},{13,9},{2,6},{6,2},{1... | collective-permute-start | bytes 1505288 | tf_op jit(solution)/shard_map/ppermute | solution.py:14
  54.0 61.0 %copy-start = (bf16[1,8,64,1120]{3,2,1,0:T(8,128)(2,1)S(1)}, bf16[1,8,64,1120]{3,2,1,0:T(8,128)(2,1)}, u32[]{:S(2)}) copy-start(bf16[1,8,64,1120]{3,2,1,0:T(8,128)(2,1)} %param.5) | copy-start | bytes 3440644
  115.0 65.3 %collective-permute-start.1 = (f32[2,10,112,112]{3,2,1,0:T(8,128)}, f32[2,10,112,112]{3,2,1,0:T(8,128)}, u32[]{:S(2)}, u32[]{:S(2)}) collective-permute-start(f32[2,10,112,112]{3,2,1,0:T(8,128)} %maximum_select_fusion.1), channel_id=1, source_target_pairs={{0,8},{4,12},{8,0},{12,4},{1,9},{5,13},{9,1},{13,5},{2,10},{6,14},... | collective-permute-start | bytes 3010568 | tf_op jit(solution)/shard_map/ppermute | solution.py:14
  180.2 3.2 %copy-start.3 = (f32[1,10,112,112]{3,2,1,0:T(8,128)S(1)}, f32[1,10,112,112]{3,2,1,0:T(8,128)}, u32[]{:S(2)}) copy-start(f32[1,10,112,112]{3,2,1,0:T(8,128)} %all-reduce.2.cloned.1.call-done) | copy-start | bytes 1505284
Sparse Core Ops, SparseCore 0:
  19.9 32.4 all-reduce.1
  192.1 11.7 reduce-scatter.1
Sparse Core Ops, SparseCore 1:
  21.8 120.9 all-gather.1
